TPU v7x, 512 devices: a whole 4x8x8 slice. The times are simulated.
512 devices in a mesh: ctx: 64 (over y, z_lo, x), mp: 8 (over z_hi, core).
Axes of the slice: x: 4, y: 8, z: 8 (z_hi: 4, z_lo: 2; z = z_hi * 2 + z_lo), core: 2. Of those that a mesh axis runs over, the one named last changes fastest.
Arguments:
- queries: bfloat16 [16384, 8192], P('ctx', 'mp'), may hold values from -6 to 6
- key_feats: bfloat16 [16384, 8192], P('ctx', 'mp'), may hold values from -6 to 6
- value_feats: bfloat16 [16384, 8192], P('ctx', 'mp'), may hold values from -6 to 6
- filters: bfloat16 [512, 128], P('mp'), may hold values from -0.5 to 0.5
- grad_out: bfloat16 [16384, 8192], P('ctx', 'mp'), may hold values from -40 to 40
Outputs:
- mixer_out: bfloat16 [16384, 8192], P('ctx', 'mp')
- grad_queries: bfloat16 [16384, 8192], P('ctx', 'mp')
- grad_keys: bfloat16 [16384, 8192], P('ctx', 'mp')
- grad_values: bfloat16 [16384, 8192], P('ctx', 'mp')
- grad_filters: float32 [512, 128], P('mp')
All inputs are finite; a program needn't handle non-finite values.
Results may differ from a plain program's by a relative error of at most 0.0058.
Values may be sent and summed in bfloat16 or wider, within the bound.
No kernel may reach another device: no remote copies, remote signals or barrier semaphores. Data moves between devices by JAX's collectives and lax.ppermute only.
A program may use at most 64 MiB of HBM per device.

v0:
```python
import jax
import jax.numpy as jnp
from jax import lax
from jax.sharding import PartitionSpec as P

D = 8192
G = 16


def contract(formula, first_op, second_op):
    return jnp.einsum(formula, first_op, second_op, preferred_element_type=jnp.float32)


def toeplitz(filt):
    count, filter_len = filt.shape
    flipped = filt[:, ::-1]
    lead_zero = jnp.zeros((count, 1), filt.dtype)
    trailing = jnp.zeros((count, filter_len), filt.dtype)
    pattern = jnp.concatenate([lead_zero, flipped, trailing], axis=1)
    repeated = jnp.tile(pattern, (1, filter_len))
    return repeated[:, : filter_len * 2 * filter_len].reshape(count, filter_len, 2 * filter_len)


def make_windows(blocks, before):
    earlier = jnp.concatenate([before[:, :, None, :], blocks[:, :, :-1, :]], axis=2)
    return jnp.concatenate([earlier, blocks], axis=3)


def forward_conv(signal, before, toeplitz_mat):
    groups_here, group_size, seq_len = signal.shape
    filter_len = toeplitz_mat.shape[1]
    blocks = signal.reshape(groups_here, group_size, seq_len // filter_len, filter_len)
    window_rows = make_windows(blocks, before)
    result = contract("gam,gsnm->gsna", toeplitz_mat, window_rows)
    return (result.reshape(groups_here, group_size, seq_len), window_rows)


def backward_conv(grad_rows, after, toeplitz_mat):
    groups_here, group_size, seq_len = grad_rows.shape
    filter_len = toeplitz_mat.shape[1]
    blocks = grad_rows.reshape(groups_here, group_size, seq_len // filter_len, filter_len)
    spread = contract("gam,gsna->gsnm", toeplitz_mat, blocks)
    tail_part = contract("gam,gsa->gsm", toeplitz_mat, after)
    next_part = jnp.concatenate(
        [spread[:, :, 1:, :filter_len], tail_part[:, :, None, :filter_len]], axis=2
    )
    return (spread[:, :, :, filter_len:] + next_part).reshape(groups_here, group_size, seq_len)


def filter_grad(grad_rows, window_rows, filter_len):
    groups_here, group_size, seq_len = grad_rows.shape
    blocks = grad_rows.reshape(groups_here, group_size, seq_len // filter_len, filter_len)
    correlate = contract("gsna,gsnm->gam", blocks, window_rows)
    flattened = correlate.reshape(groups_here, filter_len * 2 * filter_len)
    flattened = jnp.concatenate(
        [flattened, jnp.zeros((groups_here, filter_len), jnp.float32)], axis=1
    )
    flattened = flattened.reshape(groups_here, filter_len, 2 * filter_len + 1)
    diagonals = jnp.sum(flattened, axis=1)
    return diagonals[:, 1 : filter_len + 1][:, ::-1]


def shards(queries, key_feats, value_feats, filters, grad_out):
    tokens, channels = queries.shape
    slab_groups, filter_len = filters.shape
    product = (
        (key_feats.astype(jnp.float32) * value_feats.astype(jnp.float32)).astype(jnp.bfloat16).T
    )
    grad_mix = (grad_out.astype(jnp.float32) * queries.astype(jnp.float32)).astype(jnp.bfloat16).T
    owners = lax.axis_size("ctx")
    own_width = channels // owners
    own_groups = own_width // G
    signal = lax.all_to_all(product, "ctx", split_axis=0, concat_axis=1, tiled=True)
    grad_rows = lax.all_to_all(grad_mix, "ctx", split_axis=0, concat_axis=1, tiled=True)
    seq_len = signal.shape[1]
    signal = signal.reshape(own_groups, G, seq_len)
    grad_rows = grad_rows.reshape(own_groups, G, seq_len)
    first_group = lax.axis_index("ctx") * own_groups
    own_filters = lax.dynamic_slice_in_dim(filters, first_group, own_groups, 0)
    toeplitz_mat = toeplitz(own_filters)
    zero_rim = jnp.zeros((own_groups, G, filter_len), jnp.bfloat16)
    conv_out, window_rows = forward_conv(signal, zero_rim, toeplitz_mat)
    conv_out = conv_out.astype(jnp.bfloat16).reshape(own_width, seq_len)
    conv_grad = (
        backward_conv(grad_rows, zero_rim, toeplitz_mat)
        .astype(jnp.bfloat16)
        .reshape(own_width, seq_len)
    )
    partial_grad = filter_grad(grad_rows, window_rows, filter_len)
    conv_rows = lax.all_to_all(conv_out, "ctx", split_axis=1, concat_axis=0, tiled=True)
    grad_back = lax.all_to_all(conv_grad, "ctx", split_axis=1, concat_axis=0, tiled=True)
    raw_filters = lax.all_gather(partial_grad, "ctx", axis=0, tiled=True)
    conv_f = conv_rows.T.astype(jnp.float32)
    back_f = grad_back.T.astype(jnp.float32)
    mixer_out = (queries.astype(jnp.float32) * conv_f).astype(jnp.bfloat16)
    grad_queries = (grad_out.astype(jnp.float32) * conv_f).astype(jnp.bfloat16)
    grad_keys = (back_f * value_feats.astype(jnp.float32)).astype(jnp.bfloat16)
    grad_values = (back_f * key_feats.astype(jnp.float32)).astype(jnp.bfloat16)
    square_sum = lax.psum(jnp.sum(raw_filters * raw_filters), "mp")
    grad_rms = jnp.sqrt(square_sum / (D // G * filter_len) + 1e-06)
    grad_filters = raw_filters * jnp.minimum(1.0, 1.0 / grad_rms)
    return (mixer_out, grad_queries, grad_keys, grad_values, grad_filters)


def solution(mesh):
    placed = (P("ctx", "mp"), P("ctx", "mp"), P("ctx", "mp"), P("mp", None), P("ctx", "mp"))
    return jax.shard_map(
        shards,
        mesh=mesh,
        in_specs=placed,
        out_specs=(P("ctx", "mp"), P("ctx", "mp"), P("ctx", "mp"), P("ctx", "mp"), P("mp", None)),
        check_vma=False,
    )
```

profile of v0, /device:TPU:1, one launch (start us, length us, event | category | flops | bytes accessed | tf_op | source)
XLA Modules:
  0.0 278.9 jit_solution(11719873778474944530)
XLA Ops:
  0.6 1.2 copy.28
  1.9 1.2 copy.33
  3.1 0.9 fusion.6
  4.1 12.9 %all-to-all-start.2 = ((bf16[64,16,256]{2,1,0:T(8,128)(2,1)}), bf16[64,16,256]{2,1,0:T(8,128)(2,1)S(1)}, u32[]{:S(2)}, u32[]{:S(2)}) async-start(bf16[64,16,256]{2,1,0:T(8,128)(2,1)} %bitcast.10), calls=%async_computation.2 | async-start | bytes 1048576 | tf_op jit(solution)/shard_map/all_to_all | solution.py:74
  17.3 0.4 tile.13
  17.7 0.4 slice_reduce_fusion
  18.3 14.5 %all-to-all-done.2 = bf16[64,16,256]{2,1,0:T(8,128)(2,1)S(1)} async-done(((bf16[64,16,256]{2,1,0:T(8,128)(2,1)}), bf16[64,16,256]{2,1,0:T(8,128)(2,1)S(1)}, u32[]{:S(2)}, u32[]{:S(2)}) %all-to-all-start.2) | async-done | bytes 524320 | tf_op jit(solution)/shard_map/all_to_all | solution.py:74
  33.1 0.4 convolution_bitcast_fusion
  34.0 1.1 copy.35
  35.0 7.2 %all-to-all-start.3 = ((bf16[16,64,256]{2,0,1:T(8,128)(2,1)}), bf16[16,64,256]{2,0,1:T(8,128)(2,1)S(1)}, u32[]{:S(2)}, u32[]{:S(2)}) async-start(bf16[16,64,256]{2,0,1:T(8,128)(2,1)} %copy.35), calls=%async_computation.3 | async-start | bytes 1048576 | tf_op jit(solution)/shard_map/all_to_all | solution.py:91
  42.2 1.0 copy.29
  43.2 1.0 copy.30
  44.2 12.8 %all-to-all-done.3 = bf16[16,64,256]{2,0,1:T(8,128)(2,1)S(1)} async-done(((bf16[16,64,256]{2,0,1:T(8,128)(2,1)}), bf16[16,64,256]{2,0,1:T(8,128)(2,1)S(1)}, u32[]{:S(2)}, u32[]{:S(2)}) %all-to-all-start.3) | async-done | bytes 524320 | tf_op jit(solution)/shard_map/all_to_all | solution.py:91
  57.0 1.5 fusion.2
  58.5 21.8 %all_to_all.52 = bf16[64,16,256]{2,1,0:T(8,128)(2,1)S(1)} all-to-all(bf16[64,16,256]{2,1,0:T(8,128)(2,1)S(1)} %bitcast.50), channel_id=1, replica_groups=mesh['ctx'=64,'mp'=8] {'ctx'}, dimensions={0} | all-to-all | bytes 1048576 | tf_op jit(solution)/shard_map/all_to_all | solution.py:73
  80.5 1.0 reshape_reshape.2
  81.5 2.4 convolution_convert_fusion
  83.9 1.2 convert_element_type.83
  85.1 1.1 copy.32
  86.2 8.1 %all-to-all-start.1 = ((bf16[16,64,256]{2,0,1:T(8,128)(2,1)}), bf16[16,64,256]{2,0,1:T(8,128)(2,1)S(1)}, u32[]{:S(2)}, u32[]{:S(2)}) async-start(bf16[16,64,256]{2,0,1:T(8,128)(2,1)} %copy.32), calls=%async_computation.1 | async-start | bytes 1048576 | tf_op jit(solution)/shard_map/all_to_all | solution.py:90
  94.4 1.0 copy.39
  95.4 1.5 convolution_bitcast_fusion.1
  97.1 0.3 pad_reduce_fusion
  97.4 0.3 reshape.87
  97.9 127.5 %all-gather = f32[64,1,128]{2,1,0:T(1,128)S(1)} all-gather(f32[1,1,128]{2,1,0:T(1,128)S(1)} %bitcast.57), channel_id=1, replica_groups=mesh['ctx'=64,'mp'=8] {'ctx'}, dimensions={0}, use_global_device_ids=true | all-gather | bytes 33280 | tf_op jit(solution)/shard_map/all_gather | solution.py:92
  225.5 0.7 multiply_reduce_fusion
  226.1 1.0 copy.40
  227.1 48.2 %psum.7 = f32[]{:T(128)} all-reduce(f32[]{:T(128)} %multiply_reduce_fusion), channel_id=1, replica_groups=mesh['ctx'=64,'mp'=8] {'mp'}, use_global_device_ids=true, to_apply=%region_2.0 | all-reduce | flops 1 | bytes 8 | tf_op jit(solution)/shard_map/psum | solution.py:99
  276.0 0.6 broadcast_multiply_fusion
  276.6 0.2 fusion.5
  276.9 1.0 copy.37
  277.9 1.0 copy.38
  (28 shorter events, 1.7 us)
Async XLA Ops:
  0.6 16.4 %copy-start = (bf16[64,128]{1,0:T(8,128)(2,1)S(1)}, bf16[64,128]{1,0:T(8,128)(2,1)}, u32[]{:S(2)}) copy-start(bf16[64,128]{1,0:T(8,128)(2,1)} %param.8) | copy-start | bytes 49156
  4.1 28.7 %all-to-all-start.2 = ((bf16[64,16,256]{2,1,0:T(8,128)(2,1)}), bf16[64,16,256]{2,1,0:T(8,128)(2,1)S(1)}, u32[]{:S(2)}, u32[]{:S(2)}) async-start(bf16[64,16,256]{2,1,0:T(8,128)(2,1)} %bitcast.10), calls=%async_computation.2 | async-start | bytes 1048576 | tf_op jit(solution)/shard_map/all_to_all | solution.py:74
  33.8 8.5 %copy-start.1 = (bf16[256,1024]{1,0:T(8,128)(2,1)S(1)}, bf16[256,1024]{1,0:T(8,128)(2,1)}, u32[]{:S(2)}) copy-start(bf16[256,1024]{1,0:T(8,128)(2,1)} %param.6) | copy-start | bytes 1572868
  35.0 8.2 %copy-start.2 = (bf16[256,1024]{1,0:T(8,128)(2,1)S(1)}, bf16[256,1024]{1,0:T(8,128)(2,1)}, u32[]{:S(2)}) copy-start(bf16[256,1024]{1,0:T(8,128)(2,1)} %param.7) | copy-start | bytes 1572868
  35.0 22.0 %all-to-all-start.3 = ((bf16[16,64,256]{2,0,1:T(8,128)(2,1)}), bf16[16,64,256]{2,0,1:T(8,128)(2,1)S(1)}, u32[]{:S(2)}, u32[]{:S(2)}) async-start(bf16[16,64,256]{2,0,1:T(8,128)(2,1)} %copy.35), calls=%async_computation.3 | async-start | bytes 1048576 | tf_op jit(solution)/shard_map/all_to_all | solution.py:91
  86.2 190.4 %all-to-all-start.1 = ((bf16[16,64,256]{2,0,1:T(8,128)(2,1)}), bf16[16,64,256]{2,0,1:T(8,128)(2,1)S(1)}, u32[]{:S(2)}, u32[]{:S(2)}) async-start(bf16[16,64,256]{2,0,1:T(8,128)(2,1)} %copy.32), calls=%async_computation.1 | async-start | bytes 1048576 | tf_op jit(solution)/shard_map/all_to_all | solution.py:90
where the time goes:
time: 279 us
  blocking collectives  198 us (71%)
  starting transfers between devices  28.2 us (10%)
  waiting for transfers between devices  27.3 us (10%)
  local copies, waits for them, and re-layouts  15.6 us (6%)
  matrix products  4.52 us (2%)
  other arithmetic  4.21 us (2%)
    all_gather x1, blocking collectives, shards(): raw_filters = lax.all_gather(partial_grad, 'ctx', axis=0, tiled=True)  128 us
    psum x1, blocking collectives, shards(): square_sum = lax.psum(jnp.sum(raw_filters * raw_filters), 'mp')  48.2 us
    all_to_all x1, blocking collectives, shards(): lax.all_to_all(product, 'ctx', split_axis=0, concat_axis=1, tiled=True)  21.8 us
    all_to_all x1, waiting for transfers between devices, shards(): lax.all_to_all(grad_mix, 'ctx', split_axis=0, concat_axis=1, tiled=True)  14.5 us
    all_to_all x1, starting transfers between devices, shards(): lax.all_to_all(grad_mix, 'ctx', split_axis=0, concat_axis=1, tiled=True)  12.9 us
    all_to_all x1, waiting for transfers between devices, shards(): lax.all_to_all(conv_grad, 'ctx', split_axis=1, concat_axis=0, tiled=True)  12.8 us
    unnamed x15, local copies, waits for them, and re-layouts  8.66 us
    all_to_all x1, starting transfers between devices, shards(): lax.all_to_all(conv_out, 'ctx', split_axis=1, concat_axis=0, tiled=True)  8.11 us
  transfers between devices with their start and end apart: 3, of which 2 were waited for; matrix products, arithmetic and copies ran while one was open for 3% of the time, Pallas kernels for 0%

commit v1 on v0

--- a/solution.py
+++ b/solution.py
@@ -1,10 +1,21 @@
+import functools
 import jax
 import jax.numpy as jnp
 from jax import lax
 from jax.sharding import PartitionSpec as P
+from jax.lax import all_to_all, axis_size
 
 D = 8192
 G = 16
+
+
+def _state_local_data(u_in, bus_axis):
+    return jnp.concatenate(
+        all_to_all(jnp.stack([u_in] * axis_size(bus_axis)), bus_axis, 0, 0), axis=0
+    )
+
+
+group_weights = functools.partial(_state_local_data, bus_axis="ctx")
 
 
 def contract(formula, first_op, second_op):
@@ -89,7 +100,7 @@
     partial_grad = filter_grad(grad_rows, window_rows, filter_len)
     conv_rows = lax.all_to_all(conv_out, "ctx", split_axis=1, concat_axis=0, tiled=True)
     grad_back = lax.all_to_all(conv_grad, "ctx", split_axis=1, concat_axis=0, tiled=True)
-    raw_filters = lax.all_gather(partial_grad, "ctx", axis=0, tiled=True)
+    raw_filters = group_weights(partial_grad)
     conv_f = conv_rows.T.astype(jnp.float32)
     back_f = grad_back.T.astype(jnp.float32)
     mixer_out = (queries.astype(jnp.float32) * conv_f).astype(jnp.bfloat16)

time: 279 us -> 136 us (0.49)
  blocking collectives: 198 us -> 43.7 us
  starting transfers between devices: 28.2 us -> 33 us
  waiting for transfers between devices: 27.3 us -> 31.9 us
    all_gather x1 -> x0, blocking collectives: 128 us -> none  [shards(): raw_filters = lax.all_gather(partial_grad, 'ctx', axis=0, tiled=True)]
    psum x1, blocking collectives: 48.2 us -> 21.9 us  [shards(): square_sum = lax.psum(jnp.sum(raw_filters * raw_filters), 'mp')]
    all_to_all x0 -> x1, starting transfers between devices: none -> 8.1 us  [_state_local_data(): all_to_all(jnp.stack([u_in] * axis_size(bus_axis)), bus_axis, 0, 0)]
    all_to_all x0 -> x1, waiting for transfers between devices: none -> 5.68 us  [_state_local_data(): all_to_all(jnp.stack([u_in] * axis_size(bus_axis)), bus_axis, 0, 0)]
    all_to_all x1, starting transfers between devices: 8.11 us -> 4.98 us  [shards(): lax.all_to_all(conv_out, 'ctx', split_axis=1, concat_axis=0, tiled=True)]
  transfers between devices with their start and end apart: 3 -> 4, of which waited for: 2 -> 3; matrix products, arithmetic and copies ran while one was open for 3% -> 8% of each run, Pallas kernels for 0% -> 0%
where the time goes in v1:
time: 136 us; the launch traced here: 135 us
  blocking collectives  43.7 us (32%)
  starting transfers between devices  33 us (24%)
  waiting for transfers between devices  31.9 us (23%)
  local copies, waits for them, and re-layouts  17.3 us (13%)
  other arithmetic  4.21 us (3%)
  matrix products  3.36 us (2%)
  between operations  1.53 us (1%)
    psum x1, blocking collectives, shards(): square_sum = lax.psum(jnp.sum(raw_filters * raw_filters), 'mp')  21.9 us
    all_to_all x1, blocking collectives, shards(): lax.all_to_all(product, 'ctx', split_axis=0, concat_axis=1, tiled=True)  21.8 us
    all_to_all x1, waiting for transfers between devices, shards(): lax.all_to_all(grad_mix, 'ctx', split_axis=0, concat_axis=1, tiled=True)  14.5 us
    all_to_all x1, starting transfers between devices, shards(): lax.all_to_all(grad_mix, 'ctx', split_axis=0, concat_axis=1, tiled=True)  12.9 us
    all_to_all x1, waiting for transfers between devices, shards(): lax.all_to_all(conv_grad, 'ctx', split_axis=1, concat_axis=0, tiled=True)  11.8 us
    unnamed x15, local copies, waits for them, and re-layouts  9.7 us
    all_to_all x1, starting transfers between devices, _state_local_data(): all_to_all(jnp.stack([u_in] * axis_size(bus_axis)), bus_axis, 0, 0)  8.1 us
    all_to_all x1, starting transfers between devices, shards(): lax.all_to_all(conv_grad, 'ctx', split_axis=1, concat_axis=0, tiled=True)  7.03 us
  transfers between devices with their start and end apart: 4, of which 3 were waited for; matrix products, arithmetic and copies ran while one was open for 8% of the time, Pallas kernels for 0%

profile of v1, /device:TPU:1, one launch (start us, length us, event | category | flops | bytes accessed | tf_op | source)
XLA Modules:
  0.0 135.1 jit_solution(17838911074544608488)
XLA Ops:
  0.6 1.2 copy.28
  1.9 1.2 copy.33
  3.1 0.9 fusion.6
  4.1 12.9 %all-to-all-start.2 = ((bf16[64,16,256]{2,1,0:T(8,128)(2,1)}), bf16[64,16,256]{2,1,0:T(8,128)(2,1)S(1)}, u32[]{:S(2)}, u32[]{:S(2)}) async-start(bf16[64,16,256]{2,1,0:T(8,128)(2,1)} %bitcast.10), calls=%async_computation.2 | async-start | bytes 1048576 | tf_op jit(solution)/shard_map/all_to_all | solution.py:85
  17.3 0.4 tile.13
  17.7 0.4 slice_reduce_fusion
  18.3 14.5 %all-to-all-done.2 = bf16[64,16,256]{2,1,0:T(8,128)(2,1)S(1)} async-done(((bf16[64,16,256]{2,1,0:T(8,128)(2,1)}), bf16[64,16,256]{2,1,0:T(8,128)(2,1)S(1)}, u32[]{:S(2)}, u32[]{:S(2)}) %all-to-all-start.2) | async-done | bytes 524320 | tf_op jit(solution)/shard_map/all_to_all | solution.py:85
  33.1 0.4 convolution_bitcast_fusion
  34.0 1.1 copy.35
  35.0 7.0 %all-to-all-start.3 = ((bf16[16,64,256]{2,0,1:T(8,128)(2,1)}), bf16[16,64,256]{2,0,1:T(8,128)(2,1)S(1)}, u32[]{:S(2)}, u32[]{:S(2)}) async-start(bf16[16,64,256]{2,0,1:T(8,128)(2,1)} %copy.35), calls=%async_computation.3 | async-start | bytes 1048576 | tf_op jit(solution)/shard_map/all_to_all | solution.py:102
  42.1 1.0 copy.29
  43.1 2.0 %copy.30 = bf16[256,1024]{0,1:T(8,128)(2,1)} copy(bf16[256,1024]{1,0:T(8,128)(2,1)} %param.7) | data formatting | bytes 1048576 | tf_op args[2]
  45.1 11.8 %all-to-all-done.3 = bf16[16,64,256]{2,0,1:T(8,128)(2,1)S(1)} async-done(((bf16[16,64,256]{2,0,1:T(8,128)(2,1)}), bf16[16,64,256]{2,0,1:T(8,128)(2,1)S(1)}, u32[]{:S(2)}, u32[]{:S(2)}) %all-to-all-start.3) | async-done | bytes 524320 | tf_op jit(solution)/shard_map/all_to_all | solution.py:102
  56.9 1.5 %fusion.2 = (bf16[256,1024]{0,1:T(8,128)(2,1)S(1)}, bf16[256,1024]{0,1:T(8,128)(2,1)S(1)}, bf16[256,1024]{0,1:T(8,128)(2,1)S(1)}) fusion(bf16[256,1024]{0,1:T(8,128)(2,1)} %copy.29, bf16[16,64,256]{2,0,1:T(8,128)(2,1)S(1)} %all-to-all-done.3, bf16[256,1024]{0,1:T(8,128)(2,1)} %copy.30), kind=kLoop, calls=%fused_computation.13 | loop fusion | flops 2359296 | bytes 3145728 | tf_op jit(solution)/shard_map/convert_element_type | solution.py:109
  58.4 21.8 %all_to_all.57 = bf16[64,16,256]{2,1,0:T(8,128)(2,1)S(1)} all-to-all(bf16[64,16,256]{2,1,0:T(8,128)(2,1)S(1)} %bitcast.50), channel_id=1, replica_groups=mesh['ctx'=64,'mp'=8] {'ctx'}, dimensions={0} | all-to-all | bytes 1048576 | tf_op jit(solution)/shard_map/all_to_all | solution.py:84
  80.4 1.0 reshape_reshape.2
  81.4 1.6 %convolution_bitcast_fusion.1 = f32[1,1,128,256]{3,2,1,0:T(8,128)S(1)} fusion(bf16[16,128,128]{2,1,0:T(8,128)(2,1)S(1)} %reshape.92, bf16[1,16,127,128]{3,2,1,0:T(8,128)(2,1)} %bitcast.51, bf16[1,16,128,128]{3,2,1,0:T(8,128)(2,1)} %reshape_reshape.2), kind=kOutput, calls=%fused_computation.10 | convolution fusion | flops 137363456 | bytes 1699840 | tf_op jit(solution)/shard_map/gsna,gsnm->gam/dot_general | solution.py:22
  83.1 0.3 pad_reduce_fusion
  84.0 0.6 stack.2
  84.6 8.1 %all-to-all-start.4 = ((f32[64,1,128]{2,1,0:T(1,128)}), f32[64,1,128]{2,1,0:T(1,128)S(1)}, u32[]{:S(2)}, u32[]{:S(2)}) async-start(f32[64,1,128]{2,1,0:T(1,128)} %stack.2), calls=%async_computation.4 | async-start | bytes 65536 | tf_op jit(solution)/shard_map/all_to_all | solution.py:14
  92.8 1.2 convolution_convert_fusion
  94.0 1.2 convert_element_type.83
  95.2 1.1 copy.32
  96.3 5.7 %all-to-all-done.4 = f32[64,1,128]{2,1,0:T(1,128)S(1)} async-done(((f32[64,1,128]{2,1,0:T(1,128)}), f32[64,1,128]{2,1,0:T(1,128)S(1)}, u32[]{:S(2)}, u32[]{:S(2)}) %all-to-all-start.4) | async-done | bytes 32800 | tf_op jit(solution)/shard_map/all_to_all | solution.py:14
  102.0 5.0 %all-to-all-start.1 = ((bf16[16,64,256]{2,0,1:T(8,128)(2,1)}), bf16[16,64,256]{2,0,1:T(8,128)(2,1)S(1)}, u32[]{:S(2)}, u32[]{:S(2)}) async-start(bf16[16,64,256]{2,0,1:T(8,128)(2,1)} %copy.32), calls=%async_computation.1 | async-start | bytes 1048576 | tf_op jit(solution)/shard_map/all_to_all | solution.py:101
  107.0 1.0 copy.39
  108.0 0.7 multiply_reduce_fusion
  108.6 1.0 copy.40
  109.6 21.9 %psum.7 = f32[]{:T(128)} all-reduce(f32[]{:T(128)} %multiply_reduce_fusion), channel_id=1, replica_groups=mesh['ctx'=64,'mp'=8] {'mp'}, use_global_device_ids=true, to_apply=%region_2.0 | all-reduce | flops 1 | bytes 8 | tf_op jit(solution)/shard_map/psum | solution.py:110
  132.2 0.6 broadcast_multiply_fusion
  133.1 1.0 copy.37
  134.1 1.0 copy.38
  (30 shorter events, 2.3 us)
Async XLA Ops:
  0.6 16.4 %copy-start = (bf16[64,128]{1,0:T(8,128)(2,1)S(1)}, bf16[64,128]{1,0:T(8,128)(2,1)}, u32[]{:S(2)}) copy-start(bf16[64,128]{1,0:T(8,128)(2,1)} %param.8) | copy-start | bytes 49156
  4.1 28.7 %all-to-all-start.2 = ((bf16[64,16,256]{2,1,0:T(8,128)(2,1)}), bf16[64,16,256]{2,1,0:T(8,128)(2,1)S(1)}, u32[]{:S(2)}, u32[]{:S(2)}) async-start(bf16[64,16,256]{2,1,0:T(8,128)(2,1)} %bitcast.10), calls=%async_computation.2 | async-start | bytes 1048576 | tf_op jit(solution)/shard_map/all_to_all | solution.py:85
  33.9 8.1 %copy-start.1 = (bf16[256,1024]{1,0:T(8,128)(2,1)S(1)}, bf16[256,1024]{1,0:T(8,128)(2,1)}, u32[]{:S(2)}) copy-start(bf16[256,1024]{1,0:T(8,128)(2,1)} %param.6) | copy-start | bytes 1572868
  35.0 21.8 %all-to-all-start.3 = ((bf16[16,64,256]{2,0,1:T(8,128)(2,1)}), bf16[16,64,256]{2,0,1:T(8,128)(2,1)S(1)}, u32[]{:S(2)}, u32[]{:S(2)}) async-start(bf16[16,64,256]{2,0,1:T(8,128)(2,1)} %copy.35), calls=%async_computation.3 | async-start | bytes 1048576 | tf_op jit(solution)/shard_map/all_to_all | solution.py:102
  81.4 11.4 %copy-start.2 = (bf16[1,16,128,128]{3,2,1,0:T(8,128)(2,1)S(1)}, bf16[1,16,128,128]{3,2,1,0:T(8,128)(2,1)}, u32[]{:S(2)}) copy-start(bf16[1,16,128,128]{3,2,1,0:T(8,128)(2,1)} %reshape_reshape.2) | copy-start | bytes 1572868
  84.6 17.3 %all-to-all-start.4 = ((f32[64,1,128]{2,1,0:T(1,128)}), f32[64,1,128]{2,1,0:T(1,128)S(1)}, u32[]{:S(2)}, u32[]{:S(2)}) async-start(f32[64,1,128]{2,1,0:T(1,128)} %stack.2), calls=%async_computation.4 | async-start | bytes 65536 | tf_op jit(solution)/shard_map/all_to_all | solution.py:14
  102.0 30.8 %all-to-all-start.1 = ((bf16[16,64,256]{2,0,1:T(8,128)(2,1)}), bf16[16,64,256]{2,0,1:T(8,128)(2,1)S(1)}, u32[]{:S(2)}, u32[]{:S(2)}) async-start(bf16[16,64,256]{2,0,1:T(8,128)(2,1)} %copy.32), calls=%async_computation.1 | async-start | bytes 1048576 | tf_op jit(solution)/shard_map/all_to_all | solution.py:101
